TPU v7x, 32 devices: a whole 2x2x4 slice. The times are simulated.
32 devices in a mesh: freq: 8 (over z, y), tm: 4 (over x, core).
Axes of the slice: x: 2, y: 2, z: 4, core: 2. Of those that a mesh axis runs over, the one named last changes fastest.
Arguments:
- visibility: bfloat16 [8, 4, 8, 4096], P('freq', 'tm'), may hold values from -6 to 6
- model_visibility: bfloat16 [8, 4, 8, 4096], P('freq', 'tm'), may hold values from -6 to 6
- keep_mask: int32 [8, 4, 4096], P('freq', 'tm'), may hold values 0 or 1
- gains_in: float32 [8, 8, 512], P('freq'), may hold values from -6 to 6
- consensus_in: float32 [8, 8, 512], P('freq'), may hold values from -6 to 6
- dual_in: float32 [8, 8, 512], P('freq'), may hold values from -4 to 4
- penalty: float32 [512], replicated, may hold values from 30 to 600
- channel_index: int32 [8], P('freq'), may hold values from 0 to 7, each once
- first_station: int32 [4096], replicated, may hold values from 0 to 511, as said below
- second_station: int32 [4096], replicated, may hold values from 0 to 511
Outputs:
- gains_out: float32 [8, 8, 512], P('freq', None, 'tm')
- consensus_out: float32 [8, 8, 512], P('freq', None, 'tm')
- dual_out: float32 [8, 8, 512], P('freq', None, 'tm')
Inputs may be any that keep to these rules, and one draw needn't show every extreme that they name: first_station and second_station of a baseline differ; station numbers repeat over baselines. channel_index holds each channel number once.
All inputs are finite; a program needn't handle non-finite values. No bound on the sum of `keep_mask` on one device may be relied on, other than what follows from the above.
Results may differ from a plain program's by a relative error of at most 0.0003.
Values sent between devices are 32-bit elements; how exact they have to be, the bound alone decides.
No kernel may reach another device: no remote copies, remote signals or barrier semaphores. Data moves between devices by JAX's collectives and lax.ppermute only.
A program may use at most 64 MiB of HBM per device.

v0:
```python
import jax
import jax.numpy as jnp
from jax import lax
from jax.sharding import PartitionSpec as P

SWEEPS = 2


def entries(array, axis):
    return [
        (
            lax.index_in_dim(array, 2 * index, axis, False),
            lax.index_in_dim(array, 2 * index + 1, axis, False),
        )
        for index in range(4)
    ]


def stack_jones(matrix, axis):
    return jnp.stack([matrix[index][part] for index in range(4) for part in range(2)], axis=axis)


def complex_mul(leading_entry, second):
    return (
        leading_entry[0] * second[0] - leading_entry[1] * second[1],
        leading_entry[0] * second[1] + leading_entry[1] * second[0],
    )


def complex_add(leading_entry, second):
    return (leading_entry[0] + second[0], leading_entry[1] + second[1])


def matrix_mul(leading_entry, second):
    return [
        complex_add(
            complex_mul(leading_entry[0], second[0]), complex_mul(leading_entry[1], second[2])
        ),
        complex_add(
            complex_mul(leading_entry[0], second[1]), complex_mul(leading_entry[1], second[3])
        ),
        complex_add(
            complex_mul(leading_entry[2], second[0]), complex_mul(leading_entry[3], second[2])
        ),
        complex_add(
            complex_mul(leading_entry[2], second[1]), complex_mul(leading_entry[3], second[3])
        ),
    ]


def adjoint(matrix):
    return [
        (matrix[0][0], -matrix[0][1]),
        (matrix[2][0], -matrix[2][1]),
        (matrix[1][0], -matrix[1][1]),
        (matrix[3][0], -matrix[3][1]),
    ]


def weighted(matrix, weight):
    return [(entry[0] * weight, entry[1] * weight) for entry in matrix]


def one_hot_table(station_list, stations):
    return (jnp.arange(stations, dtype=jnp.int32)[:, None] == station_list[None, :]).astype(
        jnp.float32
    )


def normal_sums(vis_block, model_block, flag_block, gains, first_hot, second_hot):
    gains_first = jnp.einsum("cjs,sb->cjb", gains, first_hot, precision=lax.Precision.HIGHEST)[
        :, None
    ]
    gains_second = jnp.einsum("cjs,sb->cjb", gains, second_hot, precision=lax.Precision.HIGHEST)[
        :, None
    ]
    observed = entries(vis_block.astype(jnp.float32), 2)
    modelled = entries(model_block.astype(jnp.float32), 2)
    weight = flag_block.astype(jnp.float32)
    left = matrix_mul(modelled, adjoint(entries(gains_second, 2)))
    right = matrix_mul(adjoint(modelled), adjoint(entries(gains_first, 2)))
    num_first = weighted(matrix_mul(observed, adjoint(left)), weight)
    den_first = weighted(matrix_mul(left, adjoint(left)), weight)
    num_second = weighted(matrix_mul(adjoint(observed), adjoint(right)), weight)
    den_second = weighted(matrix_mul(right, adjoint(right)), weight)
    term_first = jnp.sum(
        jnp.concatenate([stack_jones(num_first, 1), stack_jones(den_first, 1)], axis=1), axis=2
    )
    term_second = jnp.sum(
        jnp.concatenate([stack_jones(num_second, 1), stack_jones(den_second, 1)], axis=1), axis=2
    )
    totals = jnp.einsum("cjb,sb->cjs", term_first, first_hot, precision=lax.Precision.HIGHEST)
    return totals + jnp.einsum(
        "cjb,sb->cjs", term_second, second_hot, precision=lax.Precision.HIGHEST
    )


def solve_jones(totals, gains_old, consensus, dual, penalty):
    numer = entries(totals[:, :8], 1)
    denom = entries(totals[:, 8:], 1)
    target = entries(consensus - dual, 1)
    rhs_side = [
        (numer[index][0] + penalty * target[index][0], numer[index][1] + penalty * target[index][1])
        for index in range(4)
    ]
    regular = [
        (denom[0][0] + penalty, denom[0][1]),
        denom[1],
        denom[2],
        (denom[3][0] + penalty, denom[3][1]),
    ]
    determ = complex_add(
        complex_mul(regular[0], regular[3]),
        complex_mul((-regular[1][0], -regular[1][1]), regular[2]),
    )
    magnitude = determ[0] * determ[0] + determ[1] * determ[1]
    recip = (determ[0] / magnitude, -determ[1] / magnitude)
    inverse = [
        complex_mul(regular[3], recip),
        complex_mul((-regular[1][0], -regular[1][1]), recip),
        complex_mul((-regular[2][0], -regular[2][1]), recip),
        complex_mul(regular[0], recip),
    ]
    solved = stack_jones(matrix_mul(rhs_side, inverse), 1)
    return 0.5 * (solved + gains_old)


def legendre(position):
    square = position * position
    return jnp.stack(
        [jnp.ones_like(position), position, 1.5 * square - 0.5, (2.5 * square - 1.5) * position],
        axis=-1,
    )


def channel_basis(index, total):
    return legendre(2.0 * index.astype(jnp.float32) / (total - 1.0) - 1.0)


def poly_fit(moments, total):
    basis_all = channel_basis(jnp.arange(total, dtype=jnp.int32), float(total))
    gram = jnp.dot(basis_all.T, basis_all, precision=lax.Precision.HIGHEST)
    factor = jnp.linalg.cholesky(gram)
    flat = moments.reshape(4, -1)
    middle = lax.linalg.triangular_solve(factor, flat, left_side=True, lower=True)
    coeffs = lax.linalg.triangular_solve(
        factor, middle, left_side=True, lower=True, transpose_a=True
    )
    return coeffs.reshape(moments.shape)


def shards(
    visibility,
    model_visibility,
    keep_mask,
    gains_in,
    consensus_in,
    dual_in,
    penalty,
    channel_index,
    first_station,
    second_station,
):
    stations = gains_in.shape[2]
    width = stations // lax.axis_size("tm")
    start_shift = lax.axis_index("tm") * width
    first_hot = one_hot_table(first_station, stations)
    second_hot = one_hot_table(second_station, stations)

    def own_part(array):
        return lax.dynamic_slice_in_dim(array, start_shift, width, array.ndim - 1)

    current = gains_in
    for sweep_index in range(SWEEPS):
        totals = normal_sums(
            visibility, model_visibility, keep_mask, current, first_hot, second_hot
        )
        summed = lax.psum(totals, "tm")
        current = solve_jones(summed, current, consensus_in, dual_in, penalty)
    gains_part = own_part(current)
    dual_part = own_part(dual_in)
    total_channels = channel_index.shape[0] * lax.axis_size("freq")
    basis = channel_basis(channel_index, float(total_channels))
    combined = gains_part + dual_part
    local_moments = jnp.einsum("fk,fjs->kjs", basis, combined, precision=lax.Precision.HIGHEST)
    moments = lax.psum(local_moments, "freq")
    coeffs = poly_fit(moments, total_channels)
    consensus_out = jnp.einsum("fk,kjs->fjs", basis, coeffs, precision=lax.Precision.HIGHEST)
    dual_out = dual_part + gains_part - consensus_out
    return (gains_part, consensus_out, dual_out)


def solution(mesh):
    placed = (
        P("freq", "tm", None, None),
        P("freq", "tm", None, None),
        P("freq", "tm", None),
        P("freq", None, None),
        P("freq", None, None),
        P("freq", None, None),
        P(),
        P("freq"),
        P(),
        P(),
    )
    return jax.shard_map(
        shards,
        mesh=mesh,
        in_specs=placed,
        out_specs=(P("freq", None, "tm"), P("freq", None, "tm"), P("freq", None, "tm")),
        check_vma=False,
    )
```

profile of v0, /device:TPU:0, one launch (start us, length us, event | category | flops | bytes accessed | tf_op | source)
XLA Modules:
  0.0 103.6 jit_solution(14120705225545996013)
XLA Ops:
  0.6 0.9 convert_element_type.39
  1.5 0.9 convert_element_type.40
  2.4 3.4 %fusion.10 = f32[1,1,8,4096]{3,2,1,0:T(8,128)S(1)} fusion(s32[4096]{0:T(1024)} %param.18, f32[1,8,512]{2,1,0:T(8,128)} %param.13), kind=kOutput, calls=%fused_computation.12 | convolution fusion | flops 203423744 | bytes 163840 | tf_op jit(solution)/shard_map/cjs,sb->cjb/dot_general | solution.py:71
  6.2 0.3 constant_dynamic-update-slice_fusion.29
  6.9 2.7 %fusion.8 = f32[1,1,8,4096]{3,2,1,0:T(8,128)S(1)} fusion(s32[4096]{0:T(1024)S(1)} %copy-done.8, f32[1,8,512]{2,1,0:T(8,128)S(1)} %copy-done.4), kind=kOutput, calls=%fused_computation.10 | convolution fusion | flops 203423744 | bytes 163840 | tf_op jit(solution)/shard_map/cjs,sb->cjb/dot_general | solution.py:74
  10.5 0.3 constant_dynamic-update-slice_fusion.13
  12.1 3.8 %fusion.3 = f32[16,512]{1,0:T(8,128)S(1)} fusion(s32[4096]{0:T(1024)S(1)} %copy-done.7, f32[1,16,1,4096]{3,2,1,0:T(1,128)S(1)} %constant_dynamic-update-slice_fusion), kind=kOutput, calls=%fused_computation.4 | convolution fusion | flops 404750336 | bytes 311296 | tf_op jit(solution)/shard_map/cjb,sb->cjs/dot_general | solution.py:92
  16.0 4.0 %fusion.21 = f32[1,16,512]{2,1,0:T(8,128)S(1)} fusion(f32[16,512]{1,0:T(8,128)S(1)} %fusion.3, s32[4096]{0:T(1024)S(1)} %copy-done.8, f32[1,16,1,4096]{3,2,1,0:T(1,128)S(1)} %get-tuple-element.151), kind=kOutput, calls=%fused_computation.23 | convolution fusion | flops 404758528 | bytes 344064 | tf_op jit(solution)/shard_map/cjb,sb->cjs/dot_general | solution.py:93
  20.0 12.9 %psum.21 = f32[1,16,512]{2,1,0:T(8,128)S(1)} all-reduce(f32[1,16,512]{2,1,0:T(8,128)S(1)} %fusion.21), channel_id=1, replica_groups=mesh['freq'=8,'tm'=4] {'tm'}, use_global_device_ids=true, to_apply=%region_0.0 | all-reduce | flops 8192 | bytes 65536 | tf_op jit(solution)/shard_map/psum | solution.py:178
  33.2 2.7 %fusion.11 = f32[1,1,8,4096]{3,2,1,0:T(8,128)S(1)} fusion(s32[4096]{0:T(1024)S(1)} %copy-done.7, f32[1,8,512]{2,1,0:T(8,128)S(1)} %add_multiply_fusion), kind=kOutput, calls=%fused_computation.13 | convolution fusion | flops 203423744 | bytes 163840 | tf_op jit(solution)/shard_map/cjs,sb->cjb/dot_general | solution.py:71
  36.3 0.3 constant_dynamic-update-slice_fusion.61
  37.0 2.7 %fusion.9 = f32[1,1,8,4096]{3,2,1,0:T(8,128)S(1)} fusion(s32[4096]{0:T(1024)S(1)} %copy-done.8, f32[1,8,512]{2,1,0:T(8,128)S(1)} %add_multiply_fusion), kind=kOutput, calls=%fused_computation.11 | convolution fusion | flops 203423744 | bytes 163840 | tf_op jit(solution)/shard_map/cjs,sb->cjb/dot_general | solution.py:74
  40.1 0.3 constant_dynamic-update-slice_fusion.45
  42.0 3.8 %fusion.1 = f32[16,512]{1,0:T(8,128)S(1)} fusion(s32[4096]{0:T(1024)S(1)} %copy-done.7, f32[1,16,1,4096]{3,2,1,0:T(1,128)S(1)} %constant_dynamic-update-slice_fusion.32), kind=kOutput, calls=%fused_computation.2 | convolution fusion | flops 404750336 | bytes 311296 | tf_op jit(solution)/shard_map/cjb,sb->cjs/dot_general | solution.py:92
  45.8 4.1 %fusion.23 = f32[1,16,512]{2,1,0:T(8,128)S(1)} fusion(f32[16,512]{1,0:T(8,128)S(1)} %fusion.1, s32[4096]{0:T(1024)S(1)} %copy-done.8, f32[1,16,1,4096]{3,2,1,0:T(1,128)S(1)} %get-tuple-element.139), kind=kOutput, calls=%fused_computation.25 | convolution fusion | flops 404758528 | bytes 344064 | tf_op jit(solution)/shard_map/cjb,sb->cjs/dot_general | solution.py:93
  49.9 10.3 %psum.22 = f32[1,16,512]{2,1,0:T(8,128)S(1)} all-reduce(f32[1,16,512]{2,1,0:T(8,128)S(1)} %fusion.23), channel_id=1, replica_groups=mesh['freq'=8,'tm'=4] {'tm'}, use_global_device_ids=true, to_apply=%region_1.0 | all-reduce | flops 8192 | bytes 65536 | tf_op jit(solution)/shard_map/psum | solution.py:178
  61.3 37.5 %psum.23 = f32[8,128,4]{1,0,2:T(8,128)S(1)} all-reduce(f32[8,128,4]{1,0,2:T(8,128)S(1)} %bitcast.1387), channel_id=1, replica_groups=mesh['freq'=8,'tm'=4] {'freq'}, use_global_device_ids=true, to_apply=%region_4.0 | all-reduce | flops 4096 | bytes 32768 | tf_op jit(solution)/shard_map/psum | solution.py:186
  99.1 0.4 cholesky.16
  99.6 0.7 compare_reduce_fusion
  100.2 0.6 fusion.62
  100.9 0.3 custom-call.8
  101.2 1.0 fusion.44
  102.2 0.5 fusion.65
  103.0 0.6 fusion.70
  (104 shorter events, 7.1 us)
Async XLA Ops:
  2.3 3.4 %copy-start = (s32[1,1,4096]{2,1,0:T(1,128)S(1)}, s32[1,1,4096]{2,1,0:T(1,128)}, u32[]{:S(2)}) copy-start(s32[1,1,4096]{2,1,0:T(1,128)} %param.12) | copy-start | bytes 49156
  6.2 0.7 copy-start.4
  6.2 0.7 copy-start.8
  11.4 0.7 copy-start.7
  15.9 17.0 %copy-start.2 = (f32[512]{0:T(512)S(1)}, f32[512]{0:T(512)}, u32[]{:S(2)}) copy-start(f32[512]{0:T(512)} %param.16) | copy-start | bytes 6148
  15.9 17.0 %copy-start.1 = (f32[1,8,512]{2,1,0:T(8,128)S(1)}, f32[1,8,512]{2,1,0:T(8,128)}, u32[]{:S(2)}) copy-start(f32[1,8,512]{2,1,0:T(8,128)} %param.15) | copy-start | bytes 49156
  15.9 17.0 %copy-start.3 = (f32[1,8,512]{2,1,0:T(8,128)S(1)}, f32[1,8,512]{2,1,0:T(8,128)}, u32[]{:S(2)}) copy-start(f32[1,8,512]{2,1,0:T(8,128)} %param.14) | copy-start | bytes 49156
  60.4 42.6 %copy-start.5 = (f32[1,8,128]{2,1,0:T(8,128)}, f32[1,8,128]{2,1,0:T(8,128)S(1)}, u32[]{:S(2)}) copy-start(f32[1,8,128]{2,1,0:T(8,128)S(1)} %get-tuple-element.4) | copy-start | bytes 12292
  103.0 0.6 copy-start.6
where the time goes:
time: 104 us
  blocking collectives  60.6 us (58%)
  matrix products  29.2 us (28%)
  other arithmetic  11.7 us (11%)
  between operations  1.64 us (2%)
    psum x1, blocking collectives, shards(): moments = lax.psum(local_moments, 'freq')  37.5 us
    psum x2, blocking collectives, shards(): summed = lax.psum(totals, 'tm')  23.2 us
    dot_general x2, matrix products, normal_sums(): jnp.einsum('cjb,sb->cjs', term_second, second_hot, precision=lax.Precisio...  8.11 us
    dot_general x2, matrix products, normal_sums(): jnp.einsum('cjb,sb->cjs', term_first, first_hot, precision=lax.Precision....  7.68 us
    unnamed x57, other arithmetic  6.62 us
    dot_general x2, matrix products, normal_sums(): jnp.einsum('cjs,sb->cjb', gains, first_hot, precision=lax.Precision.HIGHEST)  6.05 us
    dot_general x2, matrix products, normal_sums(): jnp.einsum('cjs,sb->cjb', gains, second_hot, precision=lax.Precision.HIGH...  5.31 us

commit v1 on v0

--- a/solution.py
+++ b/solution.py
@@ -183,7 +183,7 @@
     basis = channel_basis(channel_index, float(total_channels))
     combined = gains_part + dual_part
     local_moments = jnp.einsum("fk,fjs->kjs", basis, combined, precision=lax.Precision.HIGHEST)
-    moments = lax.psum(local_moments, "freq")
+    moments = jnp.sum(lax.all_gather(local_moments, "freq"), axis=0)
     coeffs = poly_fit(moments, total_channels)
     consensus_out = jnp.einsum("fk,kjs->fjs", basis, coeffs, precision=lax.Precision.HIGHEST)
     dual_out = dual_part + gains_part - consensus_out

time: 104 us -> 97.6 us (0.938)
  blocking collectives: 60.6 us -> 54.1 us
    psum x1 -> x0, blocking collectives: 37.5 us -> none  [shards(): moments = lax.psum(local_moments, 'freq')]
    all_gather x0 -> x1, blocking collectives: none -> 30.9 us  [shards(): moments = jnp.sum(lax.all_gather(local_moments, 'freq'), axis=0)]
    unnamed x57 -> x56, other arithmetic: 6.62 us -> 6.54 us
where the time goes in v1:
time: 97.6 us; the launch traced here: 97.1 us
  blocking collectives  54.1 us (55%)
  matrix products  29.2 us (30%)
  other arithmetic  11.7 us (12%)
  between operations  1.65 us (2%)
    all_gather x1, blocking collectives, shards(): moments = jnp.sum(lax.all_gather(local_moments, 'freq'), axis=0)  30.9 us
    psum x2, blocking collectives, shards(): summed = lax.psum(totals, 'tm')  23.2 us
    dot_general x2, matrix products, normal_sums(): jnp.einsum('cjb,sb->cjs', term_second, second_hot, precision=lax.Precisio...  8.11 us
    dot_general x2, matrix products, normal_sums(): jnp.einsum('cjb,sb->cjs', term_first, first_hot, precision=lax.Precision....  7.68 us
    unnamed x56, other arithmetic  6.54 us
    dot_general x2, matrix products, normal_sums(): jnp.einsum('cjs,sb->cjb', gains, first_hot, precision=lax.Precision.HIGHEST)  6.05 us
    dot_general x2, matrix products, normal_sums(): jnp.einsum('cjs,sb->cjb', gains, second_hot, precision=lax.Precision.HIGH...  5.31 us

profile of v1, /device:TPU:0, one launch (start us, length us, event | category | flops | bytes accessed | tf_op | source)
XLA Modules:
  0.0 97.1 jit_solution(9765739326498196158)
XLA Ops:
  0.6 0.9 convert_element_type.39
  1.5 0.9 convert_element_type.40
  2.4 3.4 %fusion.10 = f32[1,1,8,4096]{3,2,1,0:T(8,128)S(1)} fusion(s32[4096]{0:T(1024)} %param.18, f32[1,8,512]{2,1,0:T(8,128)} %param.13), kind=kOutput, calls=%fused_computation.12 | convolution fusion | flops 203423744 | bytes 163840 | tf_op jit(solution)/shard_map/cjs,sb->cjb/dot_general | solution.py:71
  6.2 0.3 constant_dynamic-update-slice_fusion.29
  6.9 2.7 %fusion.8 = f32[1,1,8,4096]{3,2,1,0:T(8,128)S(1)} fusion(s32[4096]{0:T(1024)S(1)} %copy-done.8, f32[1,8,512]{2,1,0:T(8,128)S(1)} %copy-done.4), kind=kOutput, calls=%fused_computation.10 | convolution fusion | flops 203423744 | bytes 163840 | tf_op jit(solution)/shard_map/cjs,sb->cjb/dot_general | solution.py:74
  10.5 0.3 constant_dynamic-update-slice_fusion.13
  12.1 3.8 %fusion.3 = f32[16,512]{1,0:T(8,128)S(1)} fusion(s32[4096]{0:T(1024)S(1)} %copy-done.7, f32[1,16,1,4096]{3,2,1,0:T(1,128)S(1)} %constant_dynamic-update-slice_fusion), kind=kOutput, calls=%fused_computation.4 | convolution fusion | flops 404750336 | bytes 311296 | tf_op jit(solution)/shard_map/cjb,sb->cjs/dot_general | solution.py:92
  16.0 4.0 %fusion.21 = f32[1,16,512]{2,1,0:T(8,128)S(1)} fusion(f32[16,512]{1,0:T(8,128)S(1)} %fusion.3, s32[4096]{0:T(1024)S(1)} %copy-done.8, f32[1,16,1,4096]{3,2,1,0:T(1,128)S(1)} %get-tuple-element.151), kind=kOutput, calls=%fused_computation.23 | convolution fusion | flops 404758528 | bytes 344064 | tf_op jit(solution)/shard_map/cjb,sb->cjs/dot_general | solution.py:93
  20.0 12.9 %psum.14 = f32[1,16,512]{2,1,0:T(8,128)S(1)} all-reduce(f32[1,16,512]{2,1,0:T(8,128)S(1)} %fusion.21), channel_id=1, replica_groups=mesh['freq'=8,'tm'=4] {'tm'}, use_global_device_ids=true, to_apply=%region_0.0 | all-reduce | flops 8192 | bytes 65536 | tf_op jit(solution)/shard_map/psum | solution.py:178
  33.2 2.7 %fusion.11 = f32[1,1,8,4096]{3,2,1,0:T(8,128)S(1)} fusion(s32[4096]{0:T(1024)S(1)} %copy-done.7, f32[1,8,512]{2,1,0:T(8,128)S(1)} %add_multiply_fusion), kind=kOutput, calls=%fused_computation.13 | convolution fusion | flops 203423744 | bytes 163840 | tf_op jit(solution)/shard_map/cjs,sb->cjb/dot_general | solution.py:71
  36.3 0.3 constant_dynamic-update-slice_fusion.61
  37.0 2.7 %fusion.9 = f32[1,1,8,4096]{3,2,1,0:T(8,128)S(1)} fusion(s32[4096]{0:T(1024)S(1)} %copy-done.8, f32[1,8,512]{2,1,0:T(8,128)S(1)} %add_multiply_fusion), kind=kOutput, calls=%fused_computation.11 | convolution fusion | flops 203423744 | bytes 163840 | tf_op jit(solution)/shard_map/cjs,sb->cjb/dot_general | solution.py:74
  40.1 0.3 constant_dynamic-update-slice_fusion.45
  42.0 3.8 %fusion.1 = f32[16,512]{1,0:T(8,128)S(1)} fusion(s32[4096]{0:T(1024)S(1)} %copy-done.7, f32[1,16,1,4096]{3,2,1,0:T(1,128)S(1)} %constant_dynamic-update-slice_fusion.32), kind=kOutput, calls=%fused_computation.2 | convolution fusion | flops 404750336 | bytes 311296 | tf_op jit(solution)/shard_map/cjb,sb->cjs/dot_general | solution.py:92
  45.8 4.1 %fusion.23 = f32[1,16,512]{2,1,0:T(8,128)S(1)} fusion(f32[16,512]{1,0:T(8,128)S(1)} %fusion.1, s32[4096]{0:T(1024)S(1)} %copy-done.8, f32[1,16,1,4096]{3,2,1,0:T(1,128)S(1)} %get-tuple-element.139), kind=kOutput, calls=%fused_computation.25 | convolution fusion | flops 404758528 | bytes 344064 | tf_op jit(solution)/shard_map/cjb,sb->cjs/dot_general | solution.py:93
  49.9 10.3 %psum.15 = f32[1,16,512]{2,1,0:T(8,128)S(1)} all-reduce(f32[1,16,512]{2,1,0:T(8,128)S(1)} %fusion.23), channel_id=1, replica_groups=mesh['freq'=8,'tm'=4] {'tm'}, use_global_device_ids=true, to_apply=%region_1.0 | all-reduce | flops 8192 | bytes 65536 | tf_op jit(solution)/shard_map/psum | solution.py:178
  61.3 30.9 %all-gather = f32[32,8,128]{2,1,0:T(8,128)S(1)} all-gather(f32[4,8,128]{2,1,0:T(8,128)S(1)} %broadcast_multiply_fusion), channel_id=2, replica_groups=mesh['freq'=8,'tm'=4] {'freq'}, dimensions={0}, use_global_device_ids=true | all-gather | bytes 147456 | tf_op jit(solution)/shard_map/all_gather | solution.py:186
  92.6 0.4 cholesky.16
  93.0 0.7 compare_reduce_fusion
  93.7 0.6 fusion.62
  94.3 0.3 custom-call.8
  94.7 1.0 %fusion.32 = f32[8,128,4]{2,1,0:T(8,128)S(1)} fusion(f32[1,4,8,128]{3,2,1,0:T(8,128)S(1)} %bitcast.1384, f32[1,4,4]{1,2,0:T(4,128)S(1)} %custom-call.8), kind=kOutput, calls=%fused_computation.99 | convolution fusion | flops 196608 | bytes 32832 | tf_op jit(solution)/shard_map/triangular_solve | solution.py:145
  95.7 0.5 fusion.65
  96.5 0.6 fusion.70
  (103 shorter events, 7.1 us)
Async XLA Ops:
  2.3 3.4 %copy-start = (s32[1,1,4096]{2,1,0:T(1,128)S(1)}, s32[1,1,4096]{2,1,0:T(1,128)}, u32[]{:S(2)}) copy-start(s32[1,1,4096]{2,1,0:T(1,128)} %param.12) | copy-start | bytes 49156
  6.2 0.7 copy-start.4
  6.2 0.7 copy-start.8
  11.4 0.7 copy-start.7
  15.9 17.0 %copy-start.2 = (f32[512]{0:T(512)S(1)}, f32[512]{0:T(512)}, u32[]{:S(2)}) copy-start(f32[512]{0:T(512)} %param.16) | copy-start | bytes 6148
  15.9 17.0 %copy-start.1 = (f32[1,8,512]{2,1,0:T(8,128)S(1)}, f32[1,8,512]{2,1,0:T(8,128)}, u32[]{:S(2)}) copy-start(f32[1,8,512]{2,1,0:T(8,128)} %param.15) | copy-start | bytes 49156
  15.9 17.0 %copy-start.3 = (f32[1,8,512]{2,1,0:T(8,128)S(1)}, f32[1,8,512]{2,1,0:T(8,128)}, u32[]{:S(2)}) copy-start(f32[1,8,512]{2,1,0:T(8,128)} %param.14) | copy-start | bytes 49156
  60.4 36.0 %copy-start.5 = (f32[1,8,128]{2,1,0:T(8,128)}, f32[1,8,128]{2,1,0:T(8,128)S(1)}, u32[]{:S(2)}) copy-start(f32[1,8,128]{2,1,0:T(8,128)S(1)} %get-tuple-element.4) | copy-start | bytes 12292
  96.4 0.6 copy-start.6
